TPU v7x, 128 devices: a whole 4x4x4 slice. The times are simulated.
128 devices in a mesh: req: 32 (over y, z, core), tp: 4 (over x).
Axes of the slice: x: 4, y: 4, z: 4, core: 2. Of those that a mesh axis runs over, the one named last changes fastest.
Arguments:
- states: bfloat16 [64, 512, 1024], P('req', 'tp'), may hold values from -45 to 45
- lengths: int32 [64], P('req'), may hold values from 3 to 512, as said below
- w_qkv: bfloat16 [1024, 3, 1024], P(None, None, 'tp'), may hold values from -0.1875 to 0.1875
- b_qkv: float32 [3, 1024], P(None, 'tp'), may hold values from -3 to 3
- w_out: bfloat16 [1024, 1024], P('tp'), may hold values from -0.1875 to 0.1875
- b_out: float32 [1024], replicated, may hold values from -3 to 3
- ln1_gain: float32 [1024], replicated, may hold values from 0.1 to 1.9
- ln1_shift: float32 [1024], replicated, may hold values from -3 to 3
- w_up: bfloat16 [1024, 4096], P(None, 'tp'), may hold values from -0.1875 to 0.1875
- b_up: float32 [4096], P('tp'), may hold values from -3 to 3
- w_down: bfloat16 [4096, 1024], P('tp'), may hold values from -0.09375 to 0.09375
- b_down: float32 [1024], replicated, may hold values from -3 to 3
- ln2_gain: float32 [1024], replicated, may hold values from 0.1 to 1.9
- ln2_shift: float32 [1024], replicated, may hold values from -3 to 3
- index_rows: bfloat16 [524288, 1024], P(('req', 'tp')), may hold values from -0.1875 to 0.1875
- cand_ids: int32 [64, 64], P('req', 'tp'), may hold values from 0 to 524287
Outputs:
- hidden_out: bfloat16 [64, 512, 1024], P('req', 'tp')
- scores: float32 [64, 64], P('req', 'tp')
Inputs may be any that keep to these rules, and one draw needn't show every extreme that they name: Valid positions are the first lengths ones of a text; in every draw some text has 512.
All inputs are finite; a program needn't handle non-finite values.
Results may differ from a plain program's by a relative error of at most 0.015.
Values may be sent and summed in bfloat16 or wider, within the bound.
A program may use at most 128 MiB of HBM per device.

v0:
```python
import jax
import jax.numpy as jnp
from jax import lax
from jax.sharding import PartitionSpec as P

HEAD_DIM = 64
WINDOW = 512
layer_eps = 1e-05
norm_eps = 1e-06


def layer_norm(values, gain, shift):
    centre = values - jnp.mean(values, axis=-1, keepdims=True)
    spread = jnp.mean(centre * centre, axis=-1, keepdims=True)
    return centre * lax.rsqrt(spread + layer_eps) * gain + shift


def window_attention(queries_h, keys_h, values_h, length):
    seq_len = queries_h.shape[0]
    half_window = WINDOW // 2
    padding = ((half_window, half_window), (0, 0), (0, 0))
    keys_padded = jnp.pad(keys_h, padding)
    values_padded = jnp.pad(values_h, padding)
    scale_factor = HEAD_DIM ** (-0.5)

    def one_block(block_idx):
        blk_start = block_idx * WINDOW
        query_pos = blk_start + jnp.arange(WINDOW, dtype=jnp.int32)
        key_pos = blk_start - half_window + jnp.arange(2 * WINDOW, dtype=jnp.int32)
        keep_mask = (
            (jnp.abs(query_pos[:, None] - key_pos[None, :]) <= half_window)
            & (key_pos[None, :] >= 0)
            & (key_pos[None, :] < length)
        )
        logits = (
            jnp.einsum("qhe,khe->hqk", queries_h, keys_padded, preferred_element_type=jnp.float32)
            * scale_factor
        )
        logits = jnp.where(keep_mask[None], logits, jnp.float32(-1e30))
        top_val = jnp.max(logits, axis=-1, keepdims=True)
        expo = jnp.exp(logits - top_val)
        attn_weights = (expo / jnp.sum(expo, axis=-1, keepdims=True)).astype(jnp.bfloat16)
        context = jnp.einsum(
            "hqk,khe->qhe", attn_weights, values_padded, preferred_element_type=jnp.float32
        )
        context = jnp.where((query_pos < length)[:, None, None], context, jnp.float32(0.0))
        return context.astype(jnp.bfloat16)

    blocks = lax.map(one_block, jnp.arange(seq_len // WINDOW, dtype=jnp.int32))
    return blocks.reshape(seq_len, queries_h.shape[1] * HEAD_DIM)


def per_device(
    states,
    lengths,
    w_qkv,
    b_qkv,
    w_out,
    b_out,
    ln1_gain,
    ln1_shift,
    w_up,
    b_up,
    w_down,
    b_down,
    ln2_gain,
    ln2_shift,
    index_rows,
    cand_ids,
):
    tp_count = lax.axis_size("tp")
    tp_rank = lax.axis_index("tp")
    req_count = lax.axis_size("req")
    text_count, row_share, model_width = states.shape
    full_states = lax.all_gather(states, "tp", axis=1, tiled=True)
    seq_len = full_states.shape[1]
    local_width = w_qkv.shape[2]
    heads_here = local_width // HEAD_DIM
    projected = (
        jnp.einsum("tsd,dce->tsce", full_states, w_qkv, preferred_element_type=jnp.float32) + b_qkv
    ).astype(jnp.bfloat16)
    queries_h = projected[:, :, 0].reshape(text_count, seq_len, heads_here, HEAD_DIM)
    keys_h = projected[:, :, 1].reshape(text_count, seq_len, heads_here, HEAD_DIM)
    values_h = projected[:, :, 2].reshape(text_count, seq_len, heads_here, HEAD_DIM)

    def per_text(bundle):
        return window_attention(bundle[0], bundle[1], bundle[2], bundle[3])

    context = lax.map(per_text, (queries_h, keys_h, values_h, lengths))
    partial_value = jnp.einsum("tsk,kd->tsd", context, w_out, preferred_element_type=jnp.float32)
    attn_sum = lax.psum(partial_value.astype(jnp.bfloat16), "tp").astype(jnp.float32)
    normed_full = layer_norm(
        full_states.astype(jnp.float32) + attn_sum + b_out, ln1_gain, ln1_shift
    ).astype(jnp.bfloat16)
    normed_local = lax.dynamic_slice_in_dim(normed_full, tp_rank * row_share, row_share, 1)
    up_act = jax.nn.gelu(
        jnp.einsum("tsd,df->tsf", normed_full, w_up, preferred_element_type=jnp.float32) + b_up,
        approximate=False,
    ).astype(jnp.bfloat16)
    down_part = jnp.einsum("tsf,fd->tsd", up_act, w_down, preferred_element_type=jnp.float32)
    down_sum = lax.psum_scatter(
        down_part.astype(jnp.bfloat16), "tp", scatter_dimension=1, tiled=True
    ).astype(jnp.float32)
    hidden_out = layer_norm(
        normed_local.astype(jnp.float32) + down_sum + b_down, ln2_gain, ln2_shift
    ).astype(jnp.bfloat16)
    positions = tp_rank * row_share + jnp.arange(row_share, dtype=jnp.int32)
    is_valid = positions[None, :] < lengths[:, None]
    local_pool = jnp.sum(
        jnp.where(is_valid[:, :, None], hidden_out.astype(jnp.float32), jnp.float32(0.0)), axis=1
    )
    pooled = lax.psum(local_pool, "tp") / lengths.astype(jnp.float32)[:, None]
    query_vec = (
        pooled * lax.rsqrt(jnp.mean(pooled * pooled, axis=-1, keepdims=True) + norm_eps)
    ).astype(jnp.bfloat16)
    all_queries = lax.all_gather(query_vec, "req", axis=0, tiled=True)
    quarter = cand_ids.shape[1]
    gathered_ids = lax.all_gather(cand_ids, ("req", "tp"), axis=0, tiled=True)
    all_ids = (
        gathered_ids.reshape(req_count, tp_count, text_count, quarter)
        .transpose(0, 2, 1, 3)
        .reshape(req_count * text_count, tp_count * quarter)
    )
    rows_here = index_rows.shape[0]
    first_row = (lax.axis_index("req") * tp_count + tp_rank) * rows_here
    local_ids = all_ids - first_row
    is_owned = (local_ids >= 0) & (local_ids < rows_here)
    safe_ids = jnp.clip(local_ids, 0, rows_here - 1)
    fetched = jnp.take(index_rows, safe_ids.reshape(-1), axis=0).reshape(
        safe_ids.shape[0], safe_ids.shape[1], model_width
    )
    picked = jnp.einsum("td,tcd->tc", all_queries, fetched, preferred_element_type=jnp.float32)
    owner_terms = jnp.where(is_owned, picked, jnp.float32(0.0))
    owner_terms = (
        owner_terms.reshape(req_count, text_count, tp_count, quarter)
        .transpose(0, 2, 1, 3)
        .reshape(req_count * tp_count * text_count, quarter)
    )
    scores = lax.psum_scatter(owner_terms, ("req", "tp"), scatter_dimension=0, tiled=True)
    return (hidden_out, scores)


def solution(mesh):
    placed = (
        P("req", "tp", None),
        P("req"),
        P(None, None, "tp"),
        P(None, "tp"),
        P("tp", None),
        P(),
        P(),
        P(),
        P(None, "tp"),
        P("tp"),
        P("tp", None),
        P(),
        P(),
        P(),
        P(("req", "tp"), None),
        P("req", "tp"),
    )
    return jax.shard_map(
        per_device,
        mesh=mesh,
        in_specs=placed,
        out_specs=(P("req", "tp", None), P("req", "tp")),
        check_vma=False,
    )
```

profile of v0, /device:TPU:1, one launch (start us, length us, event | category | flops | bytes accessed | tf_op | source)
XLA Modules:
  0.0 362.5 jit_solution(10841223569805811967)
XLA Ops:
  7.2 0.7 all-gather.4.cloned.1.call-update
  8.0 35.7 %all-gather.4.cloned.1.call-done = bf16[2,512,1024]{2,1,0:T(8,128)(2,1)} async-done(((bf16[2,128,1024]{2,1,0:T(8,128)(2,1)}), bf16[2,512,1024]{2,1,0:T(8,128)(2,1)}) %all-gather.4.cloned.1.call-update) | async-done | bytes 2097168 | tf_op jit(solution)/shard_map/all_gather | solution.py:75
  43.7 3.9 %add_convert_fusion.1 = bf16[2,512,3,256]{1,3,2,0:T(8,128)(2,1)S(1)} fusion(f32[3,256]{1,0:T(4,128)} %param.21, bf16[1024,3,256]{2,0,1:T(8,128)(2,1)} %param.20, bf16[2,512,1024]{2,1,0:T(8,128)(2,1)} %all-gather.4.cloned.1.call-done), kind=kOutput, calls=%fused_computation.68 | convolution fusion | flops 1612185600 | bytes 5245952 | tf_op jit(solution)/shard_map/tsd,dce->tsce/dot_general | solution.py:80
  47.6 1.2 fusion.150
  48.8 33.0 %while.17 = (s32[]{:T(128)}, bf16[2,512,256]{1,2,0:T(8,128)(2,1)}, s32[2]{0:T(128)S(1)}, bf16[2,512,4,64]{1,3,2,0:T(8,128)(2,1)}, bf16[2,512,4,64]{1,3,2,0:T(8,1...) while((s32[]{:T(128)}, bf16[2,512,256]{1,2,0:T(8,128)(2,1)}, s32[2]{0:T(128)S(1)}, ...), condition=%wide.region_3.4_spmd, body=%wide.region_0.3_spmd.sunk | while | flops 552343040 | bytes 24671904 | solution.py:89
  48.8 0.7 dynamic_slice.64
  49.5 0.7 fusion.164
  50.2 0.7 fusion.165
  50.9 1.1 dynamic-slice_bitcast_fusion.3
  52.0 6.9 %fusion.166 = (f32[4,512]{1,0:T(4,128)S(1)}, f32[4,512,1024]{2,1,0:T(8,128)}) fusion(pred[512,1024]{1,0:T(8,128)(4,1)S(1)} %fusion.165, bf16[512,4,64]{0,2,1:T(8,128)(2,1)S(1)} %get-tuple-element.195, bf16[2,512,4,64]{1,3,2,0:T(8,128)(2,1)} %get-tuple-element.217, s32[]{:T(128)} %get-tuple-element.206), kind=kOutput, calls=%fused_computation.171.clone.1 | convolution fusion | flops 276825088 | bytes 9445888 | tf_op jit(solution)/shard_map/while/body/eval_jaxpr/while/body/eval_jaxpr/sub | solution.py:41
  58.9 0.7 iota_compare_fusion.2
  59.6 4.9 %fusion.167 = bf16[4,64,512]{2,1,0:T(8,128)(2,1)S(1)} fusion(f32[4,512,1024]{2,1,0:T(8,128)} %get-tuple-element.196, f32[4,512]{1,0:T(4,128)S(1)} %get-tuple-element.197, bf16[512,4,64]{0,2,1:T(8,128)(2,1)S(1)} %get-tuple-element.198, pred[512]{0:T(512)(128)(4,1)S(1)} %iota_compare_fusion.2), kind=kOutput, calls=%fused_computation.14.clone.1 | convolution fusion | flops 272891904 | bytes 8921600 | tf_op jit(solution)/shard_map/while/body/eval_jaxpr/while/body/eval_jaxpr/hqk,khe->qhe/dot_general | solution.py:43
  64.5 0.8 copy-done.5
  65.3 0.7 dynamic_slice.64
  66.0 0.7 fusion.164
  66.7 0.7 fusion.165
  67.4 1.1 dynamic-slice_bitcast_fusion.3
  68.5 6.9 %fusion.166 = (f32[4,512]{1,0:T(4,128)S(1)}, f32[4,512,1024]{2,1,0:T(8,128)}) fusion(pred[512,1024]{1,0:T(8,128)(4,1)S(1)} %fusion.165, bf16[512,4,64]{0,2,1:T(8,128)(2,1)S(1)} %get-tuple-element.195, bf16[2,512,4,64]{1,3,2,0:T(8,128)(2,1)} %get-tuple-element.217, s32[]{:T(128)} %get-tuple-element.206), kind=kOutput, calls=%fused_computation.171.clone.1 | convolution fusion | flops 276825088 | bytes 9445888 | tf_op jit(solution)/shard_map/while/body/eval_jaxpr/while/body/eval_jaxpr/sub | solution.py:41
  75.4 0.7 iota_compare_fusion.2
  76.1 4.9 %fusion.167 = bf16[4,64,512]{2,1,0:T(8,128)(2,1)S(1)} fusion(f32[4,512,1024]{2,1,0:T(8,128)} %get-tuple-element.196, f32[4,512]{1,0:T(4,128)S(1)} %get-tuple-element.197, bf16[512,4,64]{0,2,1:T(8,128)(2,1)S(1)} %get-tuple-element.198, pred[512]{0:T(512)(128)(4,1)S(1)} %iota_compare_fusion.2), kind=kOutput, calls=%fused_computation.14.clone.1 | convolution fusion | flops 272891904 | bytes 8921600 | tf_op jit(solution)/shard_map/while/body/eval_jaxpr/while/body/eval_jaxpr/hqk,khe->qhe/dot_general | solution.py:43
  81.0 0.8 copy-done.5
  81.8 3.2 convolution_convert_fusion
  85.1 0.2 reduce-scatter.2.cloned.1.call-start
  85.3 58.6 %all-reduce.5.cloned.1.call-done = bf16[2,512,1024]{2,1,0:T(8,128)(2,1)} async-done(((bf16[2,512,1024]{2,1,0:T(8,128)(2,1)}), bf16[2,512,1024]{2,1,0:T(8,128)(2,1)}) %all-reduce.5.cloned.1.call-update) | async-done | bytes 2097168 | tf_op jit(solution)/shard_map/psum | solution.py:91
  143.9 3.1 fusion.54
  147.1 0.3 copy-done.2
  147.4 1.1 multiply_reduce_fusion
  148.5 1.2 add_convert_fusion
  149.8 3.4 fusion.103
  153.2 12.5 %fusion.92 = bf16[2,512,1024]{2,1,0:T(8,128)(2,1)} fusion(bf16[1024,1024]{1,0:T(8,128)(2,1)S(1)} %copy-done.13, f32[2,512,1024]{2,1,0:T(8,128)S(1)} %get-tuple-element.149, f32[1024]{0:T(1024)S(1)} %copy-done.14, u8[512,1024]{1,0:T(8,128)(4,1)S(1)} %get-tuple-element.123, u8[512,1024]{1,0:T(8,128)(4,1)S(1)} %get-tuple-element.122), kind=kOutput, calls=%fused_computation.105 | convolution fusion | flops 2222981120 | bytes 9441280 | tf_op jit(solution)/shard_map/tsf,fd->tsd/dot_general | solution.py:100
  165.7 55.1 %all-gather = s32[128,2,16]{2,1,0:T(2,128)S(1)} all-gather(s32[1,2,16]{2,1,0:T(2,128)S(1)} %bitcast.89), channel_id=1, replica_groups=mesh['req'=32,'tp'=4] {'req','tp'}, dimensions={0}, use_global_device_ids=true | all-gather | bytes 16512 | tf_op jit(solution)/shard_map/all_gather | solution.py:118
  220.9 0.1 subtract_clamp_fusion
  221.0 0.1 min.24
  221.2 0.1 min.22
  221.3 0.1 compare_and_fusion
  221.5 0.1 and.61
  221.7 25.4 %gather_fusion = bf16[4096,1024]{1,0:T(8,128)(2,1)} fusion(bf16[4096,1024]{1,0:T(8,128)(2,1)} %param.32, s32[4096]{0:T(1024)S(1)} %broadcast_clamp_fusion), kind=kCustom, calls=%fused_computation | custom fusion | bytes 16793600 | tf_op jit(solution)/shard_map/jit(_take)/gather | solution.py:129
  247.2 1.5 fusion.104
  248.6 1.5 multiply_reduce_fusion.1
  250.2 2.4 select_reduce_fusion
  252.6 8.4 %psum.15 = f32[2,1024]{1,0:T(2,128)S(1)} all-reduce(f32[2,1024]{1,0:T(2,128)S(1)} %get-tuple-element.138), channel_id=1, replica_groups=mesh['req'=32,'tp'=4] {'tp'}, use_global_device_ids=true, to_apply=%region_11.12 | all-reduce | flops 2048 | bytes 16384 | tf_op jit(solution)/shard_map/psum | solution.py:112
  261.0 0.2 multiply_reduce_fusion.2
  261.3 25.0 %all-gather.1 = bf16[32,2,1024]{2,1,0:T(2,128)(2,1)S(1)} all-gather(bf16[1,2,1024]{2,1,0:T(2,128)(2,1)S(1)} %fusion.108), channel_id=1, replica_groups=mesh['req'=32,'tp'=4] {'req'}, dimensions={0}, use_global_device_ids=true | all-gather | bytes 135168 | tf_op jit(solution)/shard_map/all_gather | solution.py:116
  286.3 0.1 reshape.275
  286.4 4.7 %fusion.41 = f32[64,1,64]{2,1,0:T(1,128)S(1)} fusion(bf16[64,1024,1]{1,2,0:T(2,128)(2,1)S(1)} %reshape.275, bf16[64,64,1024]{2,1,0:T(8,128)(2,1)} %bitcast.75, pred[64,64]{1,0:T(8,128)(4,1)S(1)} %compare_and_fusion.1), kind=kOutput, calls=%fused_computation.38 | convolution fusion | flops 12582912 | bytes 8540160 | tf_op jit(solution)/shard_map/td,tcd->tc/dot_general | solution.py:132
  291.2 0.1 reshape.240
  291.4 64.0 %all-reduce.2 = f32[256,16]{1,0:T(8,128)S(1)} all-reduce(f32[256,16]{1,0:T(8,128)S(1)} %bitcast.82), channel_id=3, replica_groups=mesh['req'=32,'tp'=4] {'req','tp'}, use_global_device_ids=true, to_apply=%region_13.14.clone | all-reduce | flops 4096 | bytes 32768
  355.4 0.6 constant_dynamic-slice_fusion
  (59 shorter events, 0.7 us)
Async XLA Ops:
  7.2 142.6 %copy-start = (bf16[1024,1024]{1,0:T(8,128)(2,1)S(1)}, bf16[1024,1024]{1,0:T(8,128)(2,1)}, u32[]{:S(2)}) copy-start(bf16[1024,1024]{1,0:T(8,128)(2,1)} %param.26) | copy-start | bytes 6291460
  7.2 36.5 %all-gather.4.cloned.1.call-start = ((), (), s32[]{:S(2)}) async-start(), calls=%async_computation.1 | async-start | bytes 2621440 | tf_op jit(solution)/shard_map/all_gather | solution.py:75
  7.9 136.0 %all-reduce.5.cloned.1.call-start = ((), (), s32[]{:S(2)}) async-start(), calls=%async_computation.2 | async-start | bytes 4194304 | tf_op jit(solution)/shard_map/psum | solution.py:91
  8.0 40.8 %copy-start.15 = (s32[2]{0:T(128)S(1)}, s32[2]{0:T(128)}, u32[]{:S(2)}) copy-start(s32[2]{0:T(128)} %param.19) | copy-start | bytes 28
  59.6 4.9 %copy-start.4 = (bf16[2,512,256]{1,2,0:T(8,128)(2,1)S(1)}, bf16[2,512,256]{1,2,0:T(8,128)(2,1)}, u32[]{:S(2)}) copy-start(bf16[2,512,256]{1,2,0:T(8,128)(2,1)} %get-tuple-element.207) | copy-start | bytes 1572868 | tf_op jit(solution)/shard_map/while
  64.5 0.8 copy-start.5
  76.0 4.9 %copy-start.4 = (bf16[2,512,256]{1,2,0:T(8,128)(2,1)S(1)}, bf16[2,512,256]{1,2,0:T(8,128)(2,1)}, u32[]{:S(2)}) copy-start(bf16[2,512,256]{1,2,0:T(8,128)(2,1)} %get-tuple-element.207) | copy-start | bytes 1572868 | tf_op jit(solution)/shard_map/while
  81.0 0.8 copy-start.5
  81.8 62.1 %copy-start.7 = (f32[1024]{0:T(1024)S(1)}, f32[1024]{0:T(1024)}, u32[]{:S(2)}) copy-start(f32[1024]{0:T(1024)} %param.23) | copy-start | bytes 12292
  85.1 63.4 %copy-start.10 = (f32[1024]{0:T(1024)S(1)}, f32[1024]{0:T(1024)}, u32[]{:S(2)}) copy-start(f32[1024]{0:T(1024)} %param.25) | copy-start | bytes 12292
  85.1 63.4 %copy-start.11 = (f32[1024]{0:T(1024)S(1)}, f32[1024]{0:T(1024)}, u32[]{:S(2)}) copy-start(f32[1024]{0:T(1024)} %param.24) | copy-start | bytes 12292
  85.1 162.1 %reduce-scatter.2.cloned.1.call-start = ((), (), s32[]{:S(2)}) async-start(), calls=%async_computation.3 | async-start | bytes 2621440 | tf_op jit(solution)/shard_map/reduce_scatter | solution.py:101
  143.9 3.1 copy-start.1
  143.9 3.5 copy-start.2
  148.4 1.3 copy-start.14
  149.8 3.4 copy-start.3
  149.8 3.4 copy-start.13
  153.2 12.5 %copy-start.12 = (s32[2,16]{1,0:T(2,128)S(1)}, s32[2,16]{1,0:T(2,128)}, u32[]{:S(2)}) copy-start(s32[2,16]{1,0:T(2,128)} %param.33) | copy-start | bytes 388
  221.6 25.5 %copy-start.6 = (f32[1024]{0:T(1024)S(1)}, f32[1024]{0:T(1024)}, u32[]{:S(2)}) copy-start(f32[1024]{0:T(1024)} %param.29) | copy-start | bytes 12292
  221.7 28.5 %copy-start.8 = (f32[1024]{0:T(1024)S(1)}, f32[1024]{0:T(1024)}, u32[]{:S(2)}) copy-start(f32[1024]{0:T(1024)} %param.31) | copy-start | bytes 12292
  221.7 28.5 %copy-start.9 = (f32[1024]{0:T(1024)S(1)}, f32[1024]{0:T(1024)}, u32[]{:S(2)}) copy-start(f32[1024]{0:T(1024)} %param.30) | copy-start | bytes 12292
Sparse Core Ops, SparseCore 0:
  9.7 34.0 all-gather.3
  85.2 58.6 all-reduce.4
  165.8 29.5 reduce-scatter.1
where the time goes:
time: 363 us
  blocking collectives  153 us (42%)
  waiting for transfers between devices  95 us (26%)
  matrix products  51.4 us (14%)
  local copies, waits for them, and re-layouts  33.3 us (9%)
  other arithmetic  15.6 us (4%)
  between operations  14.1 us (4%)
    unnamed x1, blocking collectives  64 us
    psum x1, waiting for transfers between devices, per_device(): lax.psum(partial_value.astype(jnp.bfloat16), 'tp').astype(jnp.float32)  58.6 us
    all_gather x1, blocking collectives, per_device(): gathered_ids = lax.all_gather(cand_ids, ('req', 'tp'), axis=0, tiled=True)  55.1 us
    all_gather x1, waiting for transfers between devices, per_device(): full_states = lax.all_gather(states, 'tp', axis=1, tiled=True)  35.7 us
    gather x1, local copies, waits for them, and re-layouts, per_device(): jnp.take(index_rows, safe_ids.reshape(-1), axis=0)  25.4 us
    all_gather x1, blocking collectives, per_device(): all_queries = lax.all_gather(query_vec, 'req', axis=0, tiled=True)  25 us
    sub x2, matrix products, one_block(): expo = jnp.exp(logits - top_val)  13.8 us
    dot_general x1, matrix products, per_device(): jnp.einsum('tsf,fd->tsd', up_act, w_down, preferred_element_type=jnp.floa...  12.5 us
  transfers between devices with their start and end apart: 3, of which 2 were waited for; matrix products, arithmetic and copies ran while one was open for 7% of the time, Pallas kernels for 0%

commit v1 on v0

--- a/solution.py
+++ b/solution.py
@@ -113,7 +113,9 @@
     query_vec = (
         pooled * lax.rsqrt(jnp.mean(pooled * pooled, axis=-1, keepdims=True) + norm_eps)
     ).astype(jnp.bfloat16)
-    all_queries = lax.all_gather(query_vec, "req", axis=0, tiled=True)
+    all_queries = jnp.concatenate(
+        lax.all_to_all(jnp.stack([query_vec] * lax.axis_size("req")), "req", 0, 0), axis=0
+    )
     quarter = cand_ids.shape[1]
     gathered_ids = lax.all_gather(cand_ids, ("req", "tp"), axis=0, tiled=True)
     all_ids = (

time: 363 us -> 352 us (0.970)
  blocking collectives: 153 us -> 127 us
  waiting for transfers between devices: 95 us -> 103 us
  starting transfers between devices: 0.3 us -> 6.52 us
    all_gather x1 -> x0, blocking collectives: 25 us -> none  [per_device(): all_queries = lax.all_gather(query_vec, 'req', axis=0, tiled=True)]
    all_to_all x0 -> x1, waiting for transfers between devices: none -> 7.79 us  [per_device(): lax.all_to_all(jnp.stack([query_vec] * lax.axis_size('req')), 'req', 0, 0)]
    all_to_all x0 -> x1, starting transfers between devices: none -> 6.22 us  [per_device(): lax.all_to_all(jnp.stack([query_vec] * lax.axis_size('req')), 'req', 0, 0)]
  transfers between devices with their start and end apart: 3 -> 4, of which waited for: 2 -> 3; matrix products, arithmetic and copies ran while one was open for 7% -> 7% of each run, Pallas kernels for 0% -> 0%
where the time goes in v1:
time: 352 us; the launch traced here: 351 us
  blocking collectives  127 us (36%)
  waiting for transfers between devices  103 us (29%)
  matrix products  51.4 us (15%)
  local copies, waits for them, and re-layouts  34.1 us (10%)
  other arithmetic  15.6 us (4%)
  between operations  14.1 us (4%)
  starting transfers between devices  6.52 us (2%)
    unnamed x1, blocking collectives  63 us
    psum x1, waiting for transfers between devices, per_device(): lax.psum(partial_value.astype(jnp.bfloat16), 'tp').astype(jnp.float32)  58.6 us
    all_gather x1, blocking collectives, per_device(): gathered_ids = lax.all_gather(cand_ids, ('req', 'tp'), axis=0, tiled=True)  55.1 us
    all_gather x1, waiting for transfers between devices, per_device(): full_states = lax.all_gather(states, 'tp', axis=1, tiled=True)  35.7 us
    gather x1, local copies, waits for them, and re-layouts, per_device(): jnp.take(index_rows, safe_ids.reshape(-1), axis=0)  25.4 us
    sub x2, matrix products, one_block(): expo = jnp.exp(logits - top_val)  13.8 us
    dot_general x1, matrix products, per_device(): jnp.einsum('tsf,fd->tsd', up_act, w_down, preferred_element_type=jnp.floa...  12.5 us
    dot_general x2, matrix products, one_block(): jnp.einsum('hqk,khe->qhe', attn_weights, values_padded, preferred_element...  9.8 us
  transfers between devices with their start and end apart: 4, of which 3 were waited for; matrix products, arithmetic and copies ran while one was open for 7% of the time, Pallas kernels for 0%

profile of v1, /device:TPU:1, one launch (start us, length us, event | category | flops | bytes accessed | tf_op | source)
XLA Modules:
  0.0 351.2 jit_solution(13242836005155999237)
XLA Ops:
  7.2 0.7 all-gather.3.cloned.1.call-update
  8.0 35.7 %all-gather.3.cloned.1.call-done = bf16[2,512,1024]{2,1,0:T(8,128)(2,1)} async-done(((bf16[2,128,1024]{2,1,0:T(8,128)(2,1)}), bf16[2,512,1024]{2,1,0:T(8,128)(2,1)}) %all-gather.3.cloned.1.call-update) | async-done | bytes 2097168 | tf_op jit(solution)/shard_map/all_gather | solution.py:75
  43.7 3.9 %add_convert_fusion.1 = bf16[2,512,3,256]{1,3,2,0:T(8,128)(2,1)S(1)} fusion(f32[3,256]{1,0:T(4,128)} %param.21, bf16[1024,3,256]{2,0,1:T(8,128)(2,1)} %param.20, bf16[2,512,1024]{2,1,0:T(8,128)(2,1)} %all-gather.3.cloned.1.call-done), kind=kOutput, calls=%fused_computation.68 | convolution fusion | flops 1612185600 | bytes 5245952 | tf_op jit(solution)/shard_map/tsd,dce->tsce/dot_general | solution.py:80
  47.6 1.2 fusion.149
  48.8 33.0 %while.17 = (s32[]{:T(128)}, bf16[2,512,256]{1,2,0:T(8,128)(2,1)}, s32[2]{0:T(128)S(1)}, bf16[2,512,4,64]{1,3,2,0:T(8,128)(2,1)}, bf16[2,512,4,64]{1,3,2,0:T(8,1...) while((s32[]{:T(128)}, bf16[2,512,256]{1,2,0:T(8,128)(2,1)}, s32[2]{0:T(128)S(1)}, ...), condition=%wide.region_3.4_spmd, body=%wide.region_0.3_spmd.sunk | while | flops 552343040 | bytes 24671904 | solution.py:89
  48.8 0.7 dynamic_slice.64
  49.5 0.7 fusion.163
  50.2 0.7 fusion.164
  50.9 1.1 dynamic-slice_bitcast_fusion.3
  52.0 6.9 %fusion.165 = (f32[4,512]{1,0:T(4,128)S(1)}, f32[4,512,1024]{2,1,0:T(8,128)}) fusion(pred[512,1024]{1,0:T(8,128)(4,1)S(1)} %fusion.164, bf16[512,4,64]{0,2,1:T(8,128)(2,1)S(1)} %get-tuple-element.195, bf16[2,512,4,64]{1,3,2,0:T(8,128)(2,1)} %get-tuple-element.217, s32[]{:T(128)} %get-tuple-element.206), kind=kOutput, calls=%fused_computation.170.clone.1 | convolution fusion | flops 276825088 | bytes 9445888 | tf_op jit(solution)/shard_map/while/body/eval_jaxpr/while/body/eval_jaxpr/sub | solution.py:41
  58.9 0.7 iota_compare_fusion.2
  59.6 4.9 %fusion.166 = bf16[4,64,512]{2,1,0:T(8,128)(2,1)S(1)} fusion(f32[4,512,1024]{2,1,0:T(8,128)} %get-tuple-element.196, f32[4,512]{1,0:T(4,128)S(1)} %get-tuple-element.197, bf16[512,4,64]{0,2,1:T(8,128)(2,1)S(1)} %get-tuple-element.198, pred[512]{0:T(512)(128)(4,1)S(1)} %iota_compare_fusion.2), kind=kOutput, calls=%fused_computation.14.clone.1 | convolution fusion | flops 272891904 | bytes 8921600 | tf_op jit(solution)/shard_map/while/body/eval_jaxpr/while/body/eval_jaxpr/hqk,khe->qhe/dot_general | solution.py:43
  64.5 0.8 copy-done.5
  65.3 0.7 dynamic_slice.64
  66.0 0.7 fusion.163
  66.7 0.7 fusion.164
  67.4 1.1 dynamic-slice_bitcast_fusion.3
  68.5 6.9 %fusion.165 = (f32[4,512]{1,0:T(4,128)S(1)}, f32[4,512,1024]{2,1,0:T(8,128)}) fusion(pred[512,1024]{1,0:T(8,128)(4,1)S(1)} %fusion.164, bf16[512,4,64]{0,2,1:T(8,128)(2,1)S(1)} %get-tuple-element.195, bf16[2,512,4,64]{1,3,2,0:T(8,128)(2,1)} %get-tuple-element.217, s32[]{:T(128)} %get-tuple-element.206), kind=kOutput, calls=%fused_computation.170.clone.1 | convolution fusion | flops 276825088 | bytes 9445888 | tf_op jit(solution)/shard_map/while/body/eval_jaxpr/while/body/eval_jaxpr/sub | solution.py:41
  75.4 0.7 iota_compare_fusion.2
  76.1 4.9 %fusion.166 = bf16[4,64,512]{2,1,0:T(8,128)(2,1)S(1)} fusion(f32[4,512,1024]{2,1,0:T(8,128)} %get-tuple-element.196, f32[4,512]{1,0:T(4,128)S(1)} %get-tuple-element.197, bf16[512,4,64]{0,2,1:T(8,128)(2,1)S(1)} %get-tuple-element.198, pred[512]{0:T(512)(128)(4,1)S(1)} %iota_compare_fusion.2), kind=kOutput, calls=%fused_computation.14.clone.1 | convolution fusion | flops 272891904 | bytes 8921600 | tf_op jit(solution)/shard_map/while/body/eval_jaxpr/while/body/eval_jaxpr/hqk,khe->qhe/dot_general | solution.py:43
  81.0 0.8 copy-done.5
  81.8 3.2 convolution_convert_fusion
  85.1 0.2 reduce-scatter.2.cloned.1.call-start
  85.3 58.6 %all-reduce.5.cloned.1.call-done = bf16[2,512,1024]{2,1,0:T(8,128)(2,1)} async-done(((bf16[2,512,1024]{2,1,0:T(8,128)(2,1)}), bf16[2,512,1024]{2,1,0:T(8,128)(2,1)}) %all-reduce.5.cloned.1.call-update) | async-done | bytes 2097168 | tf_op jit(solution)/shard_map/psum | solution.py:91
  143.9 3.1 fusion.54
  147.1 0.3 copy-done.2
  147.4 1.1 multiply_reduce_fusion
  148.5 1.2 add_convert_fusion
  149.8 3.4 fusion.103
  153.2 12.5 %fusion.92 = bf16[2,512,1024]{2,1,0:T(8,128)(2,1)} fusion(bf16[1024,1024]{1,0:T(8,128)(2,1)S(1)} %copy-done.13, f32[2,512,1024]{2,1,0:T(8,128)S(1)} %get-tuple-element.149, f32[1024]{0:T(1024)S(1)} %copy-done.14, u8[512,1024]{1,0:T(8,128)(4,1)S(1)} %get-tuple-element.123, u8[512,1024]{1,0:T(8,128)(4,1)S(1)} %get-tuple-element.122), kind=kOutput, calls=%fused_computation.105 | convolution fusion | flops 2222981120 | bytes 9441280 | tf_op jit(solution)/shard_map/tsf,fd->tsd/dot_general | solution.py:100
  165.7 55.1 %all-gather = s32[128,2,16]{2,1,0:T(2,128)S(1)} all-gather(s32[1,2,16]{2,1,0:T(2,128)S(1)} %bitcast.87), channel_id=1, replica_groups=mesh['req'=32,'tp'=4] {'req','tp'}, dimensions={0}, use_global_device_ids=true | all-gather | bytes 16512 | tf_op jit(solution)/shard_map/all_gather | solution.py:120
  221.0 0.1 min.24
  221.2 0.1 min.22
  221.3 0.1 compare_and_fusion
  221.5 0.1 and.61
  221.7 25.4 %gather_fusion = bf16[4096,1024]{1,0:T(8,128)(2,1)} fusion(bf16[4096,1024]{1,0:T(8,128)(2,1)} %param.32, s32[4096]{0:T(1024)S(1)} %broadcast_clamp_fusion), kind=kCustom, calls=%fused_computation | custom fusion | bytes 16793600 | tf_op jit(solution)/shard_map/jit(_take)/gather | solution.py:131
  247.1 1.4 fusion.104
  248.6 1.5 multiply_reduce_fusion.1
  250.1 2.4 select_reduce_fusion
  252.5 8.4 %psum.15 = f32[2,1024]{1,0:T(2,128)S(1)} all-reduce(f32[2,1024]{1,0:T(2,128)S(1)} %get-tuple-element.138), channel_id=1, replica_groups=mesh['req'=32,'tp'=4] {'tp'}, use_global_device_ids=true, to_apply=%region_11.12 | all-reduce | flops 2048 | bytes 16384 | tf_op jit(solution)/shard_map/psum | solution.py:112
  261.0 0.2 multiply_reduce_fusion.2
  261.3 0.7 stack.2
  262.0 6.2 %all-to-all-start = ((bf16[32,2,1024]{2,1,0:T(2,128)(2,1)}), bf16[32,2,1024]{2,1,0:T(2,128)(2,1)S(1)}, u32[]{:S(2)}, u32[]{:S(2)}) async-start(bf16[32,2,1024]{2,1,0:T(2,128)(2,1)} %stack.2), calls=%async_computation.1 | async-start | bytes 262144 | tf_op jit(solution)/shard_map/all_to_all | solution.py:117
  268.3 7.8 %all-to-all-done = bf16[32,2,1024]{2,1,0:T(2,128)(2,1)S(1)} async-done(((bf16[32,2,1024]{2,1,0:T(2,128)(2,1)}), bf16[32,2,1024]{2,1,0:T(2,128)(2,1)S(1)}, u32[]{:S(2)}, u32[]{:S(2)}) %all-to-all-start) | async-done | bytes 131104 | tf_op jit(solution)/shard_map/all_to_all | solution.py:117
  276.1 4.7 %fusion.41 = f32[64,1,64]{2,1,0:T(1,128)S(1)} fusion(bf16[64,1024,1]{1,2,0:T(2,128)(2,1)S(1)} %reshape.279, bf16[64,64,1024]{2,1,0:T(8,128)(2,1)} %bitcast.73, pred[64,64]{1,0:T(8,128)(4,1)S(1)} %compare_and_fusion.1), kind=kOutput, calls=%fused_computation.38 | convolution fusion | flops 12582912 | bytes 8540160 | tf_op jit(solution)/shard_map/td,tcd->tc/dot_general | solution.py:134
  280.9 0.1 reshape.246
  281.1 63.0 %all-reduce.2 = f32[256,16]{1,0:T(8,128)S(1)} all-reduce(f32[256,16]{1,0:T(8,128)S(1)} %bitcast.80), channel_id=3, replica_groups=mesh['req'=32,'tp'=4] {'req','tp'}, use_global_device_ids=true, to_apply=%region_13.14.clone | all-reduce | flops 4096 | bytes 32768
  344.1 0.6 constant_dynamic-slice_fusion
  (61 shorter events, 0.8 us)
Async XLA Ops:
  7.2 142.6 %copy-start = (bf16[1024,1024]{1,0:T(8,128)(2,1)S(1)}, bf16[1024,1024]{1,0:T(8,128)(2,1)}, u32[]{:S(2)}) copy-start(bf16[1024,1024]{1,0:T(8,128)(2,1)} %param.26) | copy-start | bytes 6291460
  7.2 36.5 %all-gather.3.cloned.1.call-start = ((), (), s32[]{:S(2)}) async-start(), calls=%async_computation.2 | async-start | bytes 2621440 | tf_op jit(solution)/shard_map/all_gather | solution.py:75
  7.9 136.0 %all-reduce.5.cloned.1.call-start = ((), (), s32[]{:S(2)}) async-start(), calls=%async_computation.3 | async-start | bytes 4194304 | tf_op jit(solution)/shard_map/psum | solution.py:91
  8.0 40.8 %copy-start.15 = (s32[2]{0:T(128)S(1)}, s32[2]{0:T(128)}, u32[]{:S(2)}) copy-start(s32[2]{0:T(128)} %param.19) | copy-start | bytes 28
  59.6 4.9 %copy-start.4 = (bf16[2,512,256]{1,2,0:T(8,128)(2,1)S(1)}, bf16[2,512,256]{1,2,0:T(8,128)(2,1)}, u32[]{:S(2)}) copy-start(bf16[2,512,256]{1,2,0:T(8,128)(2,1)} %get-tuple-element.207) | copy-start | bytes 1572868 | tf_op jit(solution)/shard_map/while
  64.5 0.8 copy-start.5
  76.0 4.9 %copy-start.4 = (bf16[2,512,256]{1,2,0:T(8,128)(2,1)S(1)}, bf16[2,512,256]{1,2,0:T(8,128)(2,1)}, u32[]{:S(2)}) copy-start(bf16[2,512,256]{1,2,0:T(8,128)(2,1)} %get-tuple-element.207) | copy-start | bytes 1572868 | tf_op jit(solution)/shard_map/while
  81.0 0.8 copy-start.5
  81.8 62.1 %copy-start.7 = (f32[1024]{0:T(1024)S(1)}, f32[1024]{0:T(1024)}, u32[]{:S(2)}) copy-start(f32[1024]{0:T(1024)} %param.23) | copy-start | bytes 12292
  85.1 63.4 %copy-start.10 = (f32[1024]{0:T(1024)S(1)}, f32[1024]{0:T(1024)}, u32[]{:S(2)}) copy-start(f32[1024]{0:T(1024)} %param.25) | copy-start | bytes 12292
  85.1 63.4 %copy-start.11 = (f32[1024]{0:T(1024)S(1)}, f32[1024]{0:T(1024)}, u32[]{:S(2)}) copy-start(f32[1024]{0:T(1024)} %param.24) | copy-start | bytes 12292
  85.1 162.0 %reduce-scatter.2.cloned.1.call-start = ((), (), s32[]{:S(2)}) async-start(), calls=%async_computation.4 | async-start | bytes 2621440 | tf_op jit(solution)/shard_map/reduce_scatter | solution.py:101
  143.9 3.1 copy-start.1
  143.9 3.5 copy-start.2
  148.4 1.3 copy-start.14
  149.8 3.4 copy-start.3
  149.8 3.4 copy-start.13
  153.2 12.5 %copy-start.12 = (s32[2,16]{1,0:T(2,128)S(1)}, s32[2,16]{1,0:T(2,128)}, u32[]{:S(2)}) copy-start(s32[2,16]{1,0:T(2,128)} %param.33) | copy-start | bytes 388
  221.6 25.5 %copy-start.6 = (f32[1024]{0:T(1024)S(1)}, f32[1024]{0:T(1024)}, u32[]{:S(2)}) copy-start(f32[1024]{0:T(1024)} %param.29) | copy-start | bytes 12292
  221.7 28.5 %copy-start.8 = (f32[1024]{0:T(1024)S(1)}, f32[1024]{0:T(1024)}, u32[]{:S(2)}) copy-start(f32[1024]{0:T(1024)} %param.31) | copy-start | bytes 12292
  221.7 28.5 %copy-start.9 = (f32[1024]{0:T(1024)S(1)}, f32[1024]{0:T(1024)}, u32[]{:S(2)}) copy-start(f32[1024]{0:T(1024)} %param.30) | copy-start | bytes 12292
  262.0 14.0 %all-to-all-start = ((bf16[32,2,1024]{2,1,0:T(2,128)(2,1)}), bf16[32,2,1024]{2,1,0:T(2,128)(2,1)S(1)}, u32[]{:S(2)}, u32[]{:S(2)}) async-start(bf16[32,2,1024]{2,1,0:T(2,128)(2,1)} %stack.2), calls=%async_computation.1 | async-start | bytes 262144 | tf_op jit(solution)/shard_map/all_to_all | solution.py:117
Sparse Core Ops, SparseCore 0:
  9.7 34.0 all-gather.2
  85.2 58.6 all-reduce.4
  165.8 29.5 reduce-scatter.1
